TPU v7x, 32 devices: a whole 2x2x4 slice. The times are simulated.
32 devices in a mesh: batch: 4 (over y, x), seq: 4 (over z), head: 2 (over core).
Axes of the slice: x: 2, y: 2, z: 4, core: 2. Of those that a mesh axis runs over, the one named last changes fastest.
Arguments:
- hidden: bfloat16 [4, 2048, 1024], P('batch', 'seq', 'head'), may hold values from -6 to 6
- norm_gain: bfloat16 [1024], P('head'), may hold values from 0.099609375 to 1.8984375
- gate_weight: bfloat16 [1024, 2048], P(None, 'head'), may hold values from -0.1875 to 0.1875
- inner_weight: bfloat16 [1024, 2048], P(None, 'head'), may hold values from -0.1875 to 0.1875
- step_weight: bfloat16 [1024, 32], P(None, 'head'), may hold values from -0.375 to 0.375
- maps_weight: bfloat16 [1024, 256], replicated, may hold values from -0.1875 to 0.1875
- inner_kernel: float32 [4, 2048], P(None, 'head'), may hold values from -3 to 3
- inner_bias: float32 [2048], P('head'), may hold values from -1 to 1
- maps_kernel: float32 [4, 256], replicated, may hold values from -3 to 3
- maps_bias: float32 [256], replicated, may hold values from -1 to 1
- step_bias: float32 [32], P('head'), may hold values from -7 to -5
- decay_log: float32 [32], P('head'), may hold values from -5.3 to 1
- skip_gain: float32 [32], P('head'), may hold values from 1 to 4
- gate_gain: float32 [2048], P('head'), may hold values from 0.1 to 1.9
- output_weight: bfloat16 [2048, 1024], P('head'), may hold values from -0.125 to 0.125
- cotangent: bfloat16 [4, 2048, 1024], P('batch', 'seq', 'head'), may hold values from -6 to 6
Outputs:
- output: float32 [4, 2048, 1024], P('batch', 'seq', 'head')
- grad_hidden: float32 [4, 2048, 1024], P('batch', 'seq', 'head')
- grad_norm_gain: float32 [1024], P('head')
- grad_gate_weight: float32 [1024, 2048], P(None, 'head')
- grad_inner_weight: float32 [1024, 2048], P(None, 'head')
- grad_step_weight: float32 [1024, 32], P(None, 'head')
- grad_maps_weight: float32 [1024, 256], replicated
- grad_inner_kernel: float32 [4, 2048], P(None, 'head')
- grad_inner_bias: float32 [2048], P('head')
- grad_maps_kernel: float32 [4, 256], replicated
- grad_maps_bias: float32 [256], replicated
- grad_step_bias: float32 [32], P('head')
- grad_decay_log: float32 [32], P('head')
- grad_skip_gain: float32 [32], P('head')
- grad_gate_gain: float32 [2048], P('head')
- grad_output_weight: float32 [2048, 1024], P('head')
All inputs are finite; a program needn't handle non-finite values.
Results may differ from a plain program's by a relative error of at most 0.0089.
Values may be sent and summed in bfloat16 or wider, within the bound.
A program may use at most 192 MiB of HBM per device.

v0:
```python
import jax
import jax.numpy as jnp
from jax import lax
from jax.sharding import PartitionSpec as P

D = 1024
HEADDIM = 64
STATE = 128
CONV = 4
GROUP = 256
DI = 2048
HIGH = lax.Precision.HIGHEST
EPSILON = 1e-05


def shifted(array, axis, by):
    count = lax.axis_size(axis)
    pairs = [(i, i + by) for i in range(count) if 0 <= i + by < count]
    return lax.ppermute(array, axis, pairs)


def entering(array, axis, combine, identity, reverse):
    count, index = (lax.axis_size(axis), lax.axis_index(axis))
    everything = jax.tree.map(lambda part: lax.all_gather(part, axis), array)
    start = jax.tree.map(
        lambda part, zero: jnp.broadcast_to(jnp.asarray(zero, part.dtype), part.shape),
        array,
        identity,
    )

    def step(k, before):
        at = count - 1 - k if reverse else k
        reached = at > index if reverse else at < index
        new = combine(before, jax.tree.map(lambda part: part[at], everything))
        return jax.tree.map(lambda a, b: jnp.where(reached, a, b), new, before)

    return lax.fori_loop(0, count, step, start)


def silu_slope(values):
    sigmoid = jax.nn.sigmoid(values)
    return sigmoid * (1.0 + values * (1.0 - sigmoid))


def ssd_blocks(inner_act, write_map, read_map, step_size, decay_rates, initial):
    length, heads, headdim = inner_act.shape
    blocks_count = length // GROUP
    inner_blocks = inner_act.reshape(blocks_count, GROUP, heads, headdim)
    write_blocks = write_map.reshape(blocks_count, GROUP, write_map.shape[-1])
    read_blocks = read_map.reshape(blocks_count, GROUP, read_map.shape[-1])
    step_blocks = step_size.reshape(blocks_count, GROUP, heads)
    causal = (jnp.arange(GROUP)[:, None] >= jnp.arange(GROUP)[None, :])[:, :, None]

    def advance(state_in, pieces):
        inner_part, write_part, read_part, step_part = pieces
        cumlog = jnp.cumsum(step_part * decay_rates[None, :], axis=0)
        spread = jnp.where(causal, cumlog[:, None, :] - cumlog[None, :, :], 0.0)
        decays = jnp.where(causal, jnp.exp(spread), 0.0)
        scores = jnp.dot(read_part, write_part.T, precision=HIGH)
        weighted = inner_part * step_part[:, :, None]
        within = jnp.einsum("tsh,shp->thp", decays * scores[:, :, None], weighted, precision=HIGH)
        carried = jnp.einsum("tn,hpn->thp", read_part, state_in, precision=HIGH)
        result = within + jnp.exp(cumlog)[:, :, None] * carried
        remain = jnp.exp(cumlog[-1][None, :] - cumlog)
        fresh = jnp.einsum("shp,sn->hpn", weighted * remain[:, :, None], write_part, precision=HIGH)
        state_out = jnp.exp(cumlog[-1])[:, None, None] * state_in + fresh
        return (state_out, result)

    final, outputs = lax.scan(
        advance, initial, (inner_blocks, write_blocks, read_blocks, step_blocks)
    )
    return (outputs.reshape(length, heads, headdim), final)


def batched_scan(inner_heads, write_map, read_map, step_size, decay_rates, state_in):
    return jax.vmap(ssd_blocks, in_axes=(0, 0, 0, 0, None, 0))(
        inner_heads, write_map, read_map, step_size, decay_rates, state_in
    )


def chain_pair(earlier, later):
    return (earlier[0] * later[0], earlier[1] * later[0][:, :, None, None] + later[1])


def conv_apply(padded, kernel, bias_row, length):
    summed = bias_row
    for offset in range(kernel.shape[0]):
        summed = summed + kernel[offset] * padded[..., offset : offset + length, :]
    return summed


def conv_grads(padded, extended, grad_out, kernel, length):
    leading = tuple(range(grad_out.ndim - 1))
    grad_kernel = jnp.stack(
        [
            jnp.sum(grad_out * padded[..., offset : offset + length, :], axis=leading)
            for offset in range(kernel.shape[0])
        ]
    )
    grad_bias = jnp.sum(grad_out, axis=leading)
    width_less = kernel.shape[0] - 1
    grad_input = jnp.zeros_like(grad_out)
    for offset in range(kernel.shape[0]):
        begin_at = width_less - offset
        grad_input = grad_input + kernel[offset] * extended[..., begin_at : begin_at + length, :]
    return (grad_input, grad_kernel, grad_bias)


def on_device(
    hidden,
    norm_gain,
    gate_weight,
    inner_weight,
    step_weight,
    maps_weight,
    inner_kernel,
    inner_bias,
    maps_kernel,
    maps_bias,
    step_bias,
    decay_log,
    skip_gain,
    gate_gain,
    output_weight,
    cotangent,
):
    seq_count, tok_count, local_width = hidden.shape
    rows_count = seq_count * tok_count
    local_inner = gate_weight.shape[1]
    heads_local = step_weight.shape[1]
    whole_hidden, whole_cotangent, whole_gain = (
        lax.all_gather(hidden, "head", axis=2, tiled=True),
        lax.all_gather(cotangent, "head", axis=2, tiled=True),
        lax.all_gather(norm_gain, "head", axis=0, tiled=True),
    )
    residual = whole_hidden.reshape(rows_count, D).astype(jnp.float32)
    inverse = lax.rsqrt(jnp.mean(residual * residual, axis=-1, keepdims=True) + EPSILON)
    normal = residual * inverse
    normed = (normal * whole_gain.astype(jnp.float32)).astype(jnp.bfloat16)
    gate_pre = jnp.dot(normed, gate_weight, preferred_element_type=jnp.float32)
    inner_pre = jnp.dot(normed, inner_weight, preferred_element_type=jnp.float32)
    maps_pre = jnp.dot(normed, maps_weight, preferred_element_type=jnp.float32)
    step_pre = jnp.dot(normed, step_weight, preferred_element_type=jnp.float32).reshape(
        seq_count, tok_count, heads_local
    )
    inner_seq = inner_pre.reshape(seq_count, tok_count, local_inner)
    maps_seq = maps_pre.reshape(seq_count, tok_count, 2 * STATE)
    edge_inner, edge_maps = shifted(
        (inner_seq[:, tok_count - (CONV - 1) :, :], maps_seq[:, tok_count - (CONV - 1) :, :]),
        "seq",
        1,
    )
    inner_pad = jnp.concatenate([edge_inner, inner_seq], axis=1)
    maps_pad = jnp.concatenate([edge_maps, maps_seq], axis=1)
    inner_conv = conv_apply(inner_pad, inner_kernel, inner_bias, tok_count)
    maps_conv = conv_apply(maps_pad, maps_kernel, maps_bias, tok_count)
    inner_act = jax.nn.silu(inner_conv)
    maps_act = jax.nn.silu(maps_conv)
    write_map = maps_act[..., :STATE]
    read_map = maps_act[..., STATE:]
    step_size = jax.nn.softplus(step_pre + step_bias)
    decay_rates = -jnp.exp(decay_log)
    inner_heads = inner_act.reshape(seq_count, tok_count, heads_local, HEADDIM)
    zero_state = jnp.zeros((seq_count, heads_local, HEADDIM, STATE), jnp.float32)
    local_mix, local_state = batched_scan(
        inner_heads, write_map, read_map, step_size, decay_rates, zero_state
    )
    cumlog = jnp.cumsum(step_size * decay_rates, axis=1)
    total_decay = jnp.exp(cumlog[:, -1, :])
    identity = (jnp.ones_like(total_decay), jnp.zeros_like(local_state))
    prefix_decay, state_in = entering(
        (total_decay, local_state), "seq", chain_pair, identity, False
    )
    carried = jnp.einsum("stn,shpn->sthp", read_map, state_in, precision=HIGH)
    mixed_out = (
        local_mix
        + jnp.exp(cumlog)[..., None] * carried
        + skip_gain[None, None, :, None] * inner_heads
    )
    mixed_flat = mixed_out.reshape(rows_count, local_inner)
    gate_act = jax.nn.silu(gate_pre)
    gated_val = mixed_flat * gate_act
    square_total = lax.psum(jnp.sum(gated_val * gated_val, axis=-1), "head")
    scale_back = lax.rsqrt(square_total[:, None] / DI + EPSILON)
    gated_norm = (gated_val * scale_back * gate_gain).astype(jnp.bfloat16)
    branch_part = jnp.dot(gated_norm, output_weight, preferred_element_type=jnp.float32)
    branch = lax.psum_scatter(branch_part, "head", scatter_dimension=1, tiled=True)
    output = (hidden.reshape(rows_count, local_width).astype(jnp.float32) + branch).reshape(
        seq_count, tok_count, local_width
    )
    cot_rows = whole_cotangent.reshape(rows_count, D)
    grad_output_weight = jnp.dot(gated_norm.T, cot_rows, preferred_element_type=jnp.float32)
    grad_norm_out = jnp.dot(cot_rows, output_weight.T, preferred_element_type=jnp.float32)
    grad_gate_gain = jnp.sum(grad_norm_out * gated_val * scale_back, axis=0)
    grad_scaled = grad_norm_out * gate_gain
    dot_total = lax.psum(jnp.sum(grad_scaled * gated_val, axis=-1), "head")
    grad_gated = scale_back * (
        grad_scaled - gated_val * scale_back * scale_back * (dot_total[:, None] / DI)
    )
    grad_mixed = (grad_gated * gate_act).reshape(seq_count, tok_count, heads_local, HEADDIM)
    grad_gate_pre = grad_gated * mixed_flat * silu_slope(gate_pre)
    grad_skip_gain = jnp.sum(grad_mixed * inner_heads, axis=(0, 1, 3))
    from_here = jnp.einsum(
        "sthp,stn->shpn", grad_mixed * jnp.exp(cumlog)[..., None], read_map, precision=HIGH
    )
    suffix_decay, state_grad = entering((total_decay, from_here), "seq", chain_pair, identity, True)
    recomputed, scan_back = jax.vjp(
        batched_scan, inner_heads, write_map, read_map, step_size, decay_rates, state_in
    )
    grad_inner_heads, grad_write, grad_read, grad_step, grad_rates, grad_start = scan_back(
        (grad_mixed, state_grad)
    )
    grad_write, grad_read = lax.psum((grad_write, grad_read), "head")
    grad_maps = jnp.concatenate([grad_write, grad_read], axis=-1)
    grad_inner = (grad_inner_heads + skip_gain[None, None, :, None] * grad_mixed).reshape(
        seq_count, tok_count, local_inner
    )
    grad_inner_conv = grad_inner * silu_slope(inner_conv)
    grad_maps_conv = grad_maps * silu_slope(maps_conv)
    next_inner, next_maps = shifted(
        (grad_inner_conv[:, : CONV - 1, :], grad_maps_conv[:, : CONV - 1, :]), "seq", -1
    )
    inner_ext = jnp.concatenate([grad_inner_conv, next_inner], axis=1)
    maps_ext = jnp.concatenate([grad_maps_conv, next_maps], axis=1)
    grad_inner_pre, grad_inner_kernel, grad_inner_bias = conv_grads(
        inner_pad, inner_ext, grad_inner_conv, inner_kernel, tok_count
    )
    grad_maps_pre, grad_maps_kernel, grad_maps_bias = conv_grads(
        maps_pad, maps_ext, grad_maps_conv, maps_kernel, tok_count
    )
    grad_step_pre = grad_step * jax.nn.sigmoid(step_pre + step_bias)
    grad_step_bias = jnp.sum(grad_step_pre, axis=(0, 1))
    grad_decay_log = grad_rates * decay_rates
    gate_round = grad_gate_pre.astype(jnp.bfloat16)
    inner_round = grad_inner_pre.reshape(rows_count, local_inner).astype(jnp.bfloat16)
    maps_round = grad_maps_pre.reshape(rows_count, 2 * STATE).astype(jnp.bfloat16)
    step_round = grad_step_pre.reshape(rows_count, heads_local).astype(jnp.bfloat16)
    grad_gate_weight = jnp.dot(normed.T, gate_round, preferred_element_type=jnp.float32)
    grad_inner_weight = jnp.dot(normed.T, inner_round, preferred_element_type=jnp.float32)
    grad_maps_weight = jnp.dot(normed.T, maps_round, preferred_element_type=jnp.float32)
    grad_step_weight = jnp.dot(normed.T, step_round, preferred_element_type=jnp.float32)
    partial_normed = jnp.dot(gate_round, gate_weight.T, preferred_element_type=jnp.float32)
    partial_normed = partial_normed + jnp.dot(
        inner_round, inner_weight.T, preferred_element_type=jnp.float32
    )
    partial_normed = partial_normed + jnp.dot(
        step_round, step_weight.T, preferred_element_type=jnp.float32
    )
    input_share = lax.psum_scatter(partial_normed, "head", scatter_dimension=1, tiled=True)
    column_start = lax.axis_index("head") * local_width
    maps_rows = lax.dynamic_slice_in_dim(maps_weight, column_start, local_width, 0)
    input_share = input_share + jnp.dot(maps_round, maps_rows.T, preferred_element_type=jnp.float32)
    normal_local = lax.dynamic_slice_in_dim(normal, column_start, local_width, 1)
    grad_normal = input_share * norm_gain.astype(jnp.float32)
    dot_sum = lax.psum(jnp.sum(grad_normal * normal_local, axis=-1), "head")
    grad_rows = inverse * (grad_normal - normal_local * (dot_sum[:, None] / D)) + cotangent.reshape(
        rows_count, local_width
    ).astype(jnp.float32)
    grad_hidden = grad_rows.reshape(seq_count, tok_count, local_width)
    grad_norm_gain = jnp.sum(input_share * normal_local, axis=0)
    summed = lax.psum(
        (
            grad_norm_gain,
            grad_gate_weight,
            grad_inner_weight,
            grad_step_weight,
            grad_maps_weight,
            grad_inner_kernel,
            grad_inner_bias,
            grad_maps_kernel,
            grad_maps_bias,
            grad_step_bias,
            grad_decay_log,
            grad_skip_gain,
            grad_gate_gain,
            grad_output_weight,
        ),
        ("batch", "seq"),
    )
    return (
        output,
        grad_hidden,
        summed[0],
        summed[1],
        summed[2],
        summed[3],
        summed[4],
        summed[5],
        summed[6],
        summed[7],
        summed[8],
        summed[9],
        summed[10],
        summed[11],
        summed[12],
        summed[13],
    )


def solution(mesh):
    return jax.shard_map(
        on_device,
        mesh=mesh,
        in_specs=(
            P("batch", "seq", "head"),
            P("head"),
            P(None, "head"),
            P(None, "head"),
            P(None, "head"),
            P(),
            P(None, "head"),
            P("head"),
            P(),
            P(),
            P("head"),
            P("head"),
            P("head"),
            P("head"),
            P("head", None),
            P("batch", "seq", "head"),
        ),
        out_specs=(
            P("batch", "seq", "head"),
            P("batch", "seq", "head"),
            P("head"),
            P(None, "head"),
            P(None, "head"),
            P(None, "head"),
            P(),
            P(None, "head"),
            P("head"),
            P(),
            P(),
            P("head"),
            P("head"),
            P("head"),
            P("head"),
            P("head", None),
        ),
        check_vma=False,
    )
```

profile of v0, /device:TPU:0, one launch (start us, length us, event | category | flops | bytes accessed | tf_op | source)
XLA Modules:
  0.0 855.7 jit_solution(2560668838805555344)
XLA Ops:
  13.6 7.7 all-gather.8.cloned.1.call-done
  24.9 3.8 collective-permute-start.1
  31.4 3.4 collective-permute-start
  43.4 3.5 reshape_reshape.7
  46.9 3.2 copy.229
  50.1 70.7 %while.120 = (s32[]{:T(128)}, f32[1,16,64,128]{3,2,1,0:T(8,128)}, f32[2,1,256,16,64]{2,0,4,3,1:T(2,128)}, f32[2,1,256,16]{2,0,3,1:T(2,128)}, f32[16]{0:T(128)S(1...) while((s32[]{:T(128)}, f32[1,16,64,128]{3,2,1,0:T(8,128)}, ...), condition=%wide.region_4.5_spmd.clone.clone, body=%wide.region_1.4_spmd.clone.clone.sunk | while | flops 1717903360 | bytes 23170916 | solution.py:69
  53.6 4.8 fusion.317
  59.5 21.9 %dynamic_update_slice.235 = f32[2,1,256,16,64]{2,0,4,3,1:T(2,128)} dynamic-update-slice(f32[2,1,256,16,64]{2,0,4,3,1:T(2,128)} %get-tuple-element.2732, f32[1,1,256,16,64]{2,0,4,3,1:T(1,128)S(1)} %copy.413, s32[]{:T(128)} %get-tuple-element.2730, s32[]{:T(128)} %constant.258.clone.1..sunk.3, s32[]{:T(128)} %constant.258.clone.1..sunk.3, s32[]{:T(128)} %constant.258.clone.1..sunk.3, ...) | dynamic-update-slice | bytes 2097156 | tf_op jit(solution)/shard_map/vmap()/while/body/jit(dynamic_update_index_in_dim)/dynamic_update_slice | solution.py:69
  81.8 3.0 fusion.313
  89.4 4.8 fusion.317
  95.3 21.9 %dynamic_update_slice.235 = f32[2,1,256,16,64]{2,0,4,3,1:T(2,128)} dynamic-update-slice(f32[2,1,256,16,64]{2,0,4,3,1:T(2,128)} %get-tuple-element.2732, f32[1,1,256,16,64]{2,0,4,3,1:T(1,128)S(1)} %copy.413, s32[]{:T(128)} %get-tuple-element.2730, s32[]{:T(128)} %constant.258.clone.1..sunk.3, s32[]{:T(128)} %constant.258.clone.1..sunk.3, s32[]{:T(128)} %constant.258.clone.1..sunk.3, ...) | dynamic-update-slice | bytes 2097156 | tf_op jit(solution)/shard_map/vmap()/while/body/jit(dynamic_update_index_in_dim)/dynamic_update_slice | solution.py:69
  117.6 3.2 fusion.313
  124.2 9.4 %all_gather.29 = f32[4,1,16]{2,1,0:T(1,128)S(1)} all-gather(f32[1,1,16]{2,1,0:T(1,128)S(1)} %exp.133), channel_id=1, replica_groups=mesh['batch'=4,'seq'=4,'head'=2] {'seq'}, dimensions={0}, use_global_device_ids=true | all-gather | bytes 320 | tf_op jit(solution)/shard_map/all_gather | solution.py:24
  138.0 3.9 transpose.187
  141.9 24.1 %all-gather.12.cloned.1.call-done = f32[4,16,64,128]{3,2,1,0:T(8,128)} async-done(((f32[1,16,64,128]{3,2,1,0:T(8,128)}), f32[4,16,64,128]{3,2,1,0:T(8,128)}) %all-gather.12.cloned.1.call-update) | async-done | bytes 2097168 | tf_op jit(solution)/shard_map/all_gather | solution.py:24
  166.0 4.8 while.118
  173.7 3.8 multiply_add_fusion
  180.4 5.5 multiply_reduce_fusion.6
  188.5 5.9 multiply_reduce_fusion
  196.8 6.6 fusion.168
  209.3 4.2 fusion.201
  220.1 46.4 %while.117 = (s32[]{:T(128)}, f32[1,16,64,128]{3,2,1,0:T(8,128)S(1)}, f32[2,1,256,256,16]{3,4,2,1,0:T(8,128)}, f32[2,1,128,256]{2,3,1,0:T(8,128)}, f32[2,1,256,1...) while((s32[]{:T(128)}, ...), condition=%wide.region_19.20_spmd.clone.clone, body=%wide.region_16.19_spmd.clone.clone.sunk | while | flops 912007232 | bytes 91645848 | solution.py:69
  225.2 6.3 multiply_dynamic-update-slice_fusion.4
  248.4 6.3 multiply_dynamic-update-slice_fusion.4
  266.5 4.5 reshape.1300
  271.0 4.5 copy.251
  275.5 7.3 while.119
  286.5 108.7 %while.121 = (s32[]{:T(128)}, f32[16]{0:T(128)}, f32[1,16,64,128]{3,2,1,0:T(8,128)S(1)}, f32[2,1,256,16,64]{2,4,3,1,0:T(8,128)}, f32[2,1,256,128]{3,2,1,0:T(8,12...) while((s32[]{:T(128)}, f32[16]{0:T(128)}, ...), condition=%wide.region_32.33_spmd.clone.clone, body=%wide.region_20.32_spmd.clone.clone.sunk | while | flops 3434913792 | bytes 128363696 | solution.py:69
  286.7 6.7 constant_dynamic-slice_fusion.20
  295.7 11.3 %fusion.331 = (f32[256,16]{0,1:T(8,128)}, f32[256,16]{0,1:T(8,128)}, f32[256,256]{1,0:T(8,128)S(1)}) fusion(f32[1,1,256,256,16]{3,4,2,1,0:T(8,128)S(1)} %constant_dynamic-slice_fusion.23, f32[256,256]{1,0:T(8,128)S(1)} %dynamic-slice_bitcast_fusion.8, pred[256,256]{1,0:T(8,128)(4,1)S(1)} %get-tuple-element.2976, ...), kind=kOutput, calls=%fused_computation.161.clone.1 | convolution fusion | flops 813621248 | bytes 11109376 | tf_op jit(solution)/shard_map/transpose(jvp(vmap()))/while/body/eval_jaxpr/tsh,shp->thp/dot_general | solution.py:61
  317.5 8.9 %fusion.330 = (f32[256,16]{0,1:T(8,128)S(1)}, f32[1,256,16,64]{1,3,2,0:T(8,128)}) fusion(f32[2,1,256,16,64]{2,4,3,1,0:T(8,128)} %get-tuple-element.2974, s32[]{:T(128)S(6)} %sub.235, f32[1,1,256,256,16]{3,4,2,1,0:T(8,128)} %get-tuple-element.2704, f32[2,1,256,16,64]{2,4,3,1,0:T(8,128)} %get-tuple-element.2960, ...), kind=kOutput, calls=%fused_computation.139.clone.1 | convolution fusion | flops 806350848 | bytes 8422400 | tf_op jit(solution)/shard_map/transpose(jvp(vmap()))/while/body/eval_jaxpr/tsh,shp->thp/dot_general | solution.py:61
  330.8 3.3 convolution_bitcast_fusion.11
  340.8 6.7 constant_dynamic-slice_fusion.20
  349.9 11.3 %fusion.331 = (f32[256,16]{0,1:T(8,128)}, f32[256,16]{0,1:T(8,128)}, f32[256,256]{1,0:T(8,128)S(1)}) fusion(f32[1,1,256,256,16]{3,4,2,1,0:T(8,128)S(1)} %constant_dynamic-slice_fusion.23, f32[256,256]{1,0:T(8,128)S(1)} %dynamic-slice_bitcast_fusion.8, pred[256,256]{1,0:T(8,128)(4,1)S(1)} %get-tuple-element.2976, ...), kind=kOutput, calls=%fused_computation.161.clone.1 | convolution fusion | flops 813621248 | bytes 11109376 | tf_op jit(solution)/shard_map/transpose(jvp(vmap()))/while/body/eval_jaxpr/tsh,shp->thp/dot_general | solution.py:61
  371.6 8.9 %fusion.330 = (f32[256,16]{0,1:T(8,128)S(1)}, f32[1,256,16,64]{1,3,2,0:T(8,128)}) fusion(f32[2,1,256,16,64]{2,4,3,1,0:T(8,128)} %get-tuple-element.2974, s32[]{:T(128)S(6)} %sub.235, f32[1,1,256,256,16]{3,4,2,1,0:T(8,128)} %get-tuple-element.2704, f32[2,1,256,16,64]{2,4,3,1,0:T(8,128)} %get-tuple-element.2960, ...), kind=kOutput, calls=%fused_computation.139.clone.1 | convolution fusion | flops 806350848 | bytes 8422400 | tf_op jit(solution)/shard_map/transpose(jvp(vmap()))/while/body/eval_jaxpr/tsh,shp->thp/dot_general | solution.py:61
  384.9 3.3 convolution_bitcast_fusion.11
  395.2 4.9 fusion.214
  404.0 4.9 copy.266
  408.8 4.9 reshape.1301
  413.8 6.4 fusion.222
  422.2 3.7 collective-permute-done.2
  431.7 4.8 fusion.218
  436.6 3.4 fusion.177
  445.1 3.4 fusion.174
  455.9 3.7 multiply_reduce_fusion.7
  462.0 81.9 %all-reduce.2 = (f32[512]{0:T(512)}, f32[4,1024]{1,0:T(4,128)}, f32[1024]{0:T(1024)}, f32[4,256]{1,0:T(4,128)}, f32[256]{0:T(256)}, /*index=5*/f32[16]{0:T(128)}, f32[16]{0:T(128)}, f32[16]{0:T(128)}, f32[1024]{0:T(1024)}) all-reduce(f32[512]{0:T(512)S(1)} %get-tuple-element.1965, ...), channel_id=1, replica_groups=mesh['batch'=4,'seq'=4,'head'=2] {'batch','seq'}, use_global_device_ids=true, to_apply=%region_39.40 | all-reduce | flops 7984 | bytes 63872 | tf_op jit(solution)/shard_map/psum | solution.py:261
  546.9 290.1 %all-reduce.8.cloned.1.call-done = (f32[1024,1024]{1,0:T(8,128)}, f32[1024,1024]{1,0:T(8,128)}, f32[1024,16]{0,1:T(8,128)}, f32[1024,256]{1,0:T(8,128)}, f32[1024,1024]{1,0:T(8,128)}) async-done(((f32[1024,1024]{1,0:T(8,128)}, f32[1024,1024]{1,0:T(8,128)}, f32[1024,16]{0,1:T(8,128)}, f32[1024,256]{1,0:T(8,128)}, f32[1024,1024]{1,0:T(8,128)}), (f32[1024,1024]{1,0:T(8,128)}, f32[1024,1024]{1,0:T(8,128)}, ...) | async-done | bytes 13697040 | tf_op jit(solution)/shard_map/psum | solution.py:261
  837.0 4.9 copy.557
  (595 shorter events, 195.1 us)
Async XLA Ops:
  7.2 173.2 %copy-start = (bf16[1024,1024]{1,0:T(8,128)(2,1)S(1)}, bf16[1024,1024]{1,0:T(8,128)(2,1)}, u32[]{:S(2)}) copy-start(bf16[1024,1024]{1,0:T(8,128)(2,1)} %param.28) | copy-start | bytes 6291460
  7.2 14.1 %all-gather.8.cloned.1.call-start = ((), (), s32[]{:S(2)}) async-start(), calls=%async_computation.2 | async-start | bytes 1572864 | tf_op jit(solution)/shard_map/all_gather | solution.py:132
  7.9 158.0 %all-gather.12.cloned.1.call-start = ((), (), s32[]{:S(2)}) async-start(), calls=%async_computation.6 | async-start | bytes 2621440 | tf_op jit(solution)/shard_map/all_gather | solution.py:24
  10.7 169.8 %copy-start.55 = (f32[2,1,512]{2,1,0:T(1,128)}, f32[2,1,512]{2,1,0:T(1,128)S(1)}, u32[]{:S(2)}) copy-start(f32[2,1,512]{2,1,0:T(1,128)S(1)} %convert_element_type.86) | copy-start | bytes 12292
  12.7 23.3 %copy-start.85 = (f32[1,256]{1,0:T(1,128)}, f32[1,256]{1,0:T(1,128)S(1)}, u32[]{:S(2)}) copy-start(f32[1,256]{1,0:T(1,128)S(1)} %get-tuple-element.2197) | copy-start | bytes 3076
  12.7 23.3 %copy-start.87 = (f32[1,256]{1,0:T(1,128)}, f32[1,256]{1,0:T(1,128)S(1)}, u32[]{:S(2)}) copy-start(f32[1,256]{1,0:T(1,128)S(1)} %get-tuple-element.2198) | copy-start | bytes 3076
  12.7 23.3 %copy-start.89 = (f32[1,256]{1,0:T(1,128)}, f32[1,256]{1,0:T(1,128)S(1)}, u32[]{:S(2)}) copy-start(f32[1,256]{1,0:T(1,128)S(1)} %get-tuple-element.2199) | copy-start | bytes 3076
  12.7 23.3 %copy-start.91 = (f32[1,256]{1,0:T(1,128)}, f32[1,256]{1,0:T(1,128)S(1)}, u32[]{:S(2)}) copy-start(f32[1,256]{1,0:T(1,128)S(1)} %get-tuple-element.2200) | copy-start | bytes 3076
  13.6 23.6 %copy-start.68 = (f32[1,1024]{1,0:T(1,128)}, f32[1,1024]{1,0:T(1,128)S(1)}, u32[]{:S(2)}) copy-start(f32[1,1024]{1,0:T(1,128)S(1)} %get-tuple-element.2193) | copy-start | bytes 12292
  13.6 23.6 %copy-start.70 = (f32[1,1024]{1,0:T(1,128)}, f32[1,1024]{1,0:T(1,128)S(1)}, u32[]{:S(2)}) copy-start(f32[1,1024]{1,0:T(1,128)S(1)} %get-tuple-element.2194) | copy-start | bytes 12292
  13.6 23.6 %copy-start.72 = (f32[1,1024]{1,0:T(1,128)}, f32[1,1024]{1,0:T(1,128)S(1)}, u32[]{:S(2)}) copy-start(f32[1,1024]{1,0:T(1,128)S(1)} %get-tuple-element.2195) | copy-start | bytes 12292
  13.6 23.6 %copy-start.74 = (f32[1,1024]{1,0:T(1,128)}, f32[1,1024]{1,0:T(1,128)S(1)}, u32[]{:S(2)}) copy-start(f32[1,1024]{1,0:T(1,128)S(1)} %get-tuple-element.2196) | copy-start | bytes 12292
  21.3 7.4 copy-start.24
  21.3 7.4 copy-start.41
  23.0 157.4 %copy-start.63 = (f32[512]{0:T(512)}, f32[512]{0:T(512)S(1)}, u32[]{:S(2)}) copy-start(f32[512]{0:T(512)S(1)} %add_rsqrt_fusion.1) | copy-start | bytes 6148
  24.9 11.1 %copy-start.30 = (f32[512,256]{1,0:T(8,128)}, f32[512,256]{1,0:T(8,128)S(1)}, u32[]{:S(2)}) copy-start(f32[512,256]{1,0:T(8,128)S(1)} %fusion.220) | copy-start | bytes 1572868
  24.9 9.9 %copy-start.76 = (bf16[1024,16]{0,1:T(8,128)(2,1)S(1)}, bf16[1024,16]{0,1:T(8,128)(2,1)}, u32[]{:S(2)}) copy-start(bf16[1024,16]{0,1:T(8,128)(2,1)} %param.30) | copy-start | bytes 98308
  24.9 9.9 %copy-start.100 = (f32[16]{0:T(128)S(1)}, f32[16]{0:T(128)}, u32[]{:S(2)}) copy-start(f32[16]{0:T(128)} %param.36) | copy-start | bytes 196
  24.9 11.0 %collective-permute-start.1 = (f32[1,3,256]{2,1,0:T(4,128)S(1)}, f32[1,3,256]{2,1,0:T(4,128)S(1)}, u32[]{:S(2)}, u32[]{:S(2)}) collective-permute-start(f32[1,3,256]{2,1,0:T(4,128)S(1)} %slice.201), channel_id=1, source_target_pairs={{0,2},{2,4},{4,6},{1,3},{3,5},{5,7},{8,10},{10,12},{12,14},{9,11},... | collective-permute-start | bytes 9224 | tf_op jit(solution)/shard_map/ppermute | solution.py:19
  31.4 5.8 collective-permute-start
  120.8 67.6 %all-gather.10.cloned.1.call-start = ((), (), s32[]{:S(2)}) async-start(), calls=%async_computation.4 | async-start | bytes 1572864 | tf_op jit(solution)/shard_map/all_gather | solution.py:133
  121.6 154.0 %all-gather.14.cloned.1.call-start = ((), (), s32[]{:S(2)}) async-start(), calls=%async_computation.7 | async-start | bytes 2621440 | tf_op jit(solution)/shard_map/all_gather | solution.py:24
  180.4 8.0 copy-start.61
  188.4 8.4 copy-start.78
  196.8 7.9 copy-start.31
  213.6 227.5 %all-reduce.10.cloned.1.call-start = ((), (), s32[]{:S(2)}) async-start(), calls=%async_computation.9 | async-start | bytes 1048576 | tf_op jit(solution)/shard_map/psum | solution.py:213
  225.2 7.3 copy-start.21
  235.8 7.4 copy-start.50
  236.0 7.3 copy-start.53
  248.4 7.3 copy-start.21
  259.0 7.4 copy-start.50
  259.2 7.3 copy-start.53
  317.5 13.2 %copy-start.57 = (f32[2,1,256,16,1]{2,0,4,3,1:T(2,128)S(1)}, f32[2,1,256,16,1]{2,0,4,3,1:T(2,128)}, u32[]{:S(2)}) copy-start(f32[2,1,256,16,1]{2,0,4,3,1:T(2,128)} %get-tuple-element.2966) | copy-start | bytes 98308 | tf_op jit(solution)/shard_map/transpose(jvp(vmap()))/while
  329.3 7.3 copy-start.47
  330.8 7.7 copy-start.5
  371.6 13.2 %copy-start.57 = (f32[2,1,256,16,1]{2,0,4,3,1:T(2,128)S(1)}, f32[2,1,256,16,1]{2,0,4,3,1:T(2,128)}, u32[]{:S(2)}) copy-start(f32[2,1,256,16,1]{2,0,4,3,1:T(2,128)} %get-tuple-element.2966) | copy-start | bytes 98308 | tf_op jit(solution)/shard_map/transpose(jvp(vmap()))/while
  383.5 7.3 copy-start.23
  383.5 7.3 copy-start.47
  384.9 7.7 copy-start.5
  395.2 58.2 %reduce-scatter.3.cloned.1.call-start = ((), (), s32[]{:S(2)}) async-start(), calls=%async_computation.3 | async-start | bytes 3145728 | tf_op jit(solution)/shard_map/reduce_scatter | solution.py:187
  400.2 55.8 %reduce-scatter.5.cloned.1.call-start = ((), (), s32[]{:S(2)}) async-start(), calls=%async_computation.5 | async-start | bytes 3145728 | tf_op jit(solution)/shard_map/reduce_scatter | solution.py:249
  413.7 7.8 copy-start.60
  413.8 7.8 copy-start.59
  413.8 8.0 copy-start.77
  420.3 5.6 collective-permute-start.2
  430.5 406.5 %all-reduce.8.cloned.1.call-start = ((), (), s32[]{:S(2)}) async-start(), calls=%async_computation.8 | async-start | bytes 27394048 | tf_op jit(solution)/shard_map/psum | solution.py:261
  443.6 5.5 collective-permute-start.3
  455.9 88.0 %copy-start.35 = (f32[512,512]{1,0:T(8,128)S(1)}, f32[512,512]{1,0:T(8,128)}, u32[]{:S(2)}) copy-start(f32[512,512]{1,0:T(8,128)} %reduce-scatter.5.cloned.1.call-done) | copy-start | bytes 3145732
  (108 other events, 385.6 us)
Sparse Core Ops, SparseCore 0:
  9.5 11.7 all-gather.7
  121.0 44.9 all-gather.11
  167.5 7.8 all-gather.9
  213.7 44.5 all-gather.13
  395.3 17.5 all-reduce.9
  415.0 10.8 reduce-scatter.2
  430.6 8.5 reduce-scatter.4
  451.1 385.9 all-reduce.7
where the time goes:
time: 872 us; the launch traced here: 856 us
  waiting for transfers between devices  328 us (38%)
  local copies, waits for them, and re-layouts  169 us (19%)
  matrix products  141 us (16%)
  blocking collectives  101 us (12%)
  other arithmetic  90.1 us (10%)
  between operations  15.5 us (2%)
  starting transfers between devices  10.8 us (1%)
    psum x1, waiting for transfers between devices, on_device(): lax.psum((grad_norm_gain, grad_gate_weight, grad_inner_weight, grad_step_...  290 us
    psum x1, blocking collectives, on_device(): lax.psum((grad_norm_gain, grad_gate_weight, grad_inner_weight, grad_step_...  81.9 us
    dynamic_update_slice x24, local copies, waits for them, and re-layouts, ssd_blocks(): lax.scan(advance, initial, (inner_blocks, write_blocks, read_blocks, step...  63.8 us
    dot_general x6, matrix products, advance(): jnp.einsum('tsh,shp->thp', decays * scores[:, :, None], weighted, precisi...  50 us
    unnamed x150, local copies, waits for them, and re-layouts  26.9 us
    all_gather x2, waiting for transfers between devices, entering(): everything = jax.tree.map(lambda part: lax.all_gather(part, axis), array)  24.1 us
    dynamic_slice x18, local copies, waits for them, and re-layouts, ssd_blocks(): lax.scan(advance, initial, (inner_blocks, write_blocks, read_blocks, step...  17.4 us
  transfers between devices with their start and end apart: 12, of which 5 were waited for; matrix products, arithmetic and copies ran while one was open for 18% of the time, Pallas kernels for 0%

commit v1 on v0

--- a/solution.py
+++ b/solution.py
@@ -2,6 +2,7 @@
 import jax.numpy as jnp
 from jax import lax
 from jax.sharding import PartitionSpec as P
+from jax.lax import psum
 
 D = 1024
 HEADDIM = 64
@@ -11,6 +12,12 @@
 DI = 2048
 HIGH = lax.Precision.HIGHEST
 EPSILON = 1e-05
+
+
+def _assign_pairs_all(inputs):
+    for h in ("batch", "seq"):
+        inputs = psum(inputs, h)
+    return inputs
 
 
 def shifted(array, axis, by):
@@ -258,7 +265,7 @@
     ).astype(jnp.float32)
     grad_hidden = grad_rows.reshape(seq_count, tok_count, local_width)
     grad_norm_gain = jnp.sum(input_share * normal_local, axis=0)
-    summed = lax.psum(
+    summed = _assign_pairs_all(
         (
             grad_norm_gain,
             grad_gate_weight,
@@ -274,8 +281,7 @@
             grad_skip_gain,
             grad_gate_gain,
             grad_output_weight,
-        ),
-        ("batch", "seq"),
+        )
     )
     return (
         output,

time: 872 us -> 1240 us (1.42)
  waiting for transfers between devices: 328 us -> 734 us
  blocking collectives: 101 us -> 58.9 us
    psum x1 -> x2, waiting for transfers between devices: 290 us -> 667 us  [_assign_pairs_all(): inputs = psum(inputs, h)]
    psum x1 -> x2, blocking collectives: 81.9 us -> 40.3 us  [_assign_pairs_all(): inputs = psum(inputs, h)]
    unnamed x150 -> x152, local copies, waits for them, and re-layouts: 26.9 us -> 26.5 us
  transfers between devices with their start and end apart: 12 -> 13, of which waited for: 5 -> 9; matrix products, arithmetic and copies ran while one was open for 18% -> 11% of each run, Pallas kernels for 0% -> 0%
where the time goes in v1:
time: 1240 us; the launch traced here: 1220 us
  waiting for transfers between devices  734 us (59%)
  local copies, waits for them, and re-layouts  171 us (14%)
  matrix products  140 us (11%)
  other arithmetic  91.5 us (7%)
  blocking collectives  58.9 us (5%)
  between operations  15.2 us (1%)
    psum x2, waiting for transfers between devices, _assign_pairs_all(): inputs = psum(inputs, h)  667 us
    dynamic_update_slice x24, local copies, waits for them, and re-layouts, ssd_blocks(): lax.scan(advance, initial, (inner_blocks, write_blocks, read_blocks, step...  63.8 us
    dot_general x6, matrix products, advance(): jnp.einsum('tsh,shp->thp', decays * scores[:, :, None], weighted, precisi...  50 us
    psum x2, blocking collectives, _assign_pairs_all(): inputs = psum(inputs, h)  40.3 us
    unnamed x152, local copies, waits for them, and re-layouts  26.5 us
  transfers between devices with their start and end apart: 13, of which 9 were waited for; matrix products, arithmetic and copies ran while one was open for 11% of the time, Pallas kernels for 0%

profile of v1, /device:TPU:0, one launch (start us, length us, event | category | flops | bytes accessed | tf_op | source)
XLA Modules:
  0.0 1222.9 jit_solution(11248333143010310421)
XLA Ops:
  13.6 7.7 all-gather.8.cloned.1.call-done
  24.9 3.8 collective-permute-start.1
  31.4 3.4 collective-permute-start
  43.3 3.5 reshape_reshape.7
  50.0 70.7 %while.120 = (s32[]{:T(128)}, f32[1,16,64,128]{3,2,1,0:T(8,128)}, f32[2,1,256,16,64]{2,0,4,3,1:T(2,128)}, f32[2,1,256,16]{2,0,3,1:T(2,128)}, f32[16]{0:T(128)S(1...) while((s32[]{:T(128)}, f32[1,16,64,128]{3,2,1,0:T(8,128)}, ...), condition=%wide.region_4.5_spmd.clone.clone, body=%wide.region_1.4_spmd.clone.clone.sunk | while | flops 1717903360 | bytes 23170916 | solution.py:76
  53.5 4.8 fusion.317
  59.4 21.9 %dynamic_update_slice.235 = f32[2,1,256,16,64]{2,0,4,3,1:T(2,128)} dynamic-update-slice(f32[2,1,256,16,64]{2,0,4,3,1:T(2,128)} %get-tuple-element.2746, f32[1,1,256,16,64]{2,0,4,3,1:T(1,128)S(1)} %copy.413, s32[]{:T(128)} %get-tuple-element.2744, s32[]{:T(128)} %constant.258.clone.1..sunk.3, s32[]{:T(128)} %constant.258.clone.1..sunk.3, s32[]{:T(128)} %constant.258.clone.1..sunk.3, ...) | dynamic-update-slice | bytes 2097156 | tf_op jit(solution)/shard_map/vmap()/while/body/jit(dynamic_update_index_in_dim)/dynamic_update_slice | solution.py:76
  89.3 4.8 fusion.317
  95.2 21.9 %dynamic_update_slice.235 = f32[2,1,256,16,64]{2,0,4,3,1:T(2,128)} dynamic-update-slice(f32[2,1,256,16,64]{2,0,4,3,1:T(2,128)} %get-tuple-element.2746, f32[1,1,256,16,64]{2,0,4,3,1:T(1,128)S(1)} %copy.413, s32[]{:T(128)} %get-tuple-element.2744, s32[]{:T(128)} %constant.258.clone.1..sunk.3, s32[]{:T(128)} %constant.258.clone.1..sunk.3, s32[]{:T(128)} %constant.258.clone.1..sunk.3, ...) | dynamic-update-slice | bytes 2097156 | tf_op jit(solution)/shard_map/vmap()/while/body/jit(dynamic_update_index_in_dim)/dynamic_update_slice | solution.py:76
  124.8 9.3 all_gather.29
  138.7 3.9 transpose.187
  142.6 23.3 %all-gather.12.cloned.1.call-done = f32[4,16,64,128]{3,2,1,0:T(8,128)} async-done(((f32[1,16,64,128]{3,2,1,0:T(8,128)}), f32[4,16,64,128]{3,2,1,0:T(8,128)}) %all-gather.12.cloned.1.call-update) | async-done | bytes 2097168 | tf_op jit(solution)/shard_map/all_gather | solution.py:31
  165.9 4.8 while.118
  173.7 3.8 multiply_add_fusion
  180.4 5.5 multiply_reduce_fusion.6
  188.4 5.9 multiply_reduce_fusion
  196.7 6.6 fusion.168
  209.2 4.2 fusion.201
  220.0 46.4 %while.117 = (s32[]{:T(128)}, f32[1,16,64,128]{3,2,1,0:T(8,128)S(1)}, f32[2,1,256,256,16]{3,4,2,1,0:T(8,128)}, f32[2,1,128,256]{2,3,1,0:T(8,128)}, f32[2,1,256,1...) while((s32[]{:T(128)}, ...), condition=%wide.region_19.20_spmd.clone.clone, body=%wide.region_16.19_spmd.clone.clone.sunk | while | flops 912007232 | bytes 91645848 | solution.py:76
  225.1 6.2 multiply_dynamic-update-slice_fusion.4
  248.3 6.3 multiply_dynamic-update-slice_fusion.4
  266.4 4.5 reshape.1300
  270.9 4.5 copy.251
  275.5 5.1 fusion.218
  280.6 3.4 fusion.177
  284.0 7.4 while.119
  295.2 106.7 %while.121 = (s32[]{:T(128)}, f32[16]{0:T(128)}, f32[1,16,64,128]{3,2,1,0:T(8,128)S(1)}, f32[2,1,256,16,64]{2,4,3,1,0:T(8,128)}, f32[2,1,256,128]{3,2,1,0:T(8,12...) while((s32[]{:T(128)}, f32[16]{0:T(128)}, ...), condition=%wide.region_32.33_spmd.clone.clone, body=%wide.region_20.32_spmd.clone.clone.sunk | while | flops 3434913792 | bytes 128233152 | solution.py:76
  295.3 6.7 constant_dynamic-slice_fusion.20
  304.4 11.3 fusion.331
  326.2 8.9 fusion.330
  348.5 6.7 constant_dynamic-slice_fusion.20
  357.6 11.3 fusion.331
  379.4 8.9 fusion.330
  391.6 3.3 convolution_bitcast_fusion.11
  401.9 4.9 copy.266
  406.7 4.9 reshape.1301
  411.6 6.8 fusion.222
  425.4 5.7 fusion.162
  431.2 9.9 all-reduce.15.cloned.1.call-done
  445.1 3.4 fusion.174
  451.8 4.9 fusion.214
  463.5 247.3 %all-reduce.13.cloned.1.call-done = (f32[1024,1024]{1,0:T(8,128)}, f32[1024,1024]{1,0:T(8,128)}, f32[1024,16]{0,1:T(8,128)}, f32[1024,256]{1,0:T(8,128)}, f32[1024,1024]{1,0:T(8,128)}) async-done(((f32[1024,1024]{1,0:T(8,128)}, f32[1024,1024]{1,0:T(8,128)}, f32[1024,16]{0,1:T(8,128)}, f32[1024,256]{1,0:T(8,128)}, f32[1024,1024]{1,0:T(8,128)}), (f32[1024,1024]{1,0:T(8,128)}, f32[1024,1024]{1,0:T(8,128)}, ...) | async-done | bytes 13697040 | tf_op jit(solution)/shard_map/psum | solution.py:19
  713.2 10.1 reduce-scatter.3.cloned.1.call-done
  725.8 10.7 reduce-scatter.5.cloned.1.call-done
  739.5 17.0 %all-reduce.4 = (f32[512]{0:T(512)S(1)}, f32[4,1024]{1,0:T(4,128)S(1)}, f32[1024]{0:T(1024)S(1)}, f32[4,256]{1,0:T(4,128)S(1)}, f32[256]{0:T(256)S(1)}, /*index=...) all-reduce(f32[512]{0:T(512)S(1)} %get-tuple-element.1965, ...), channel_id=1, replica_groups=mesh['batch'=4,'seq'=4,'head'=2] {'batch'}, use_global_device_ids=true, to_apply=%region_39.40 | all-reduce | flops 7984 | bytes 63872 | tf_op jit(solution)/shard_map/psum | solution.py:19
  759.0 23.3 %all-reduce.2 = (f32[512]{0:T(512)}, f32[4,1024]{1,0:T(4,128)}, f32[1024]{0:T(1024)}, f32[4,256]{1,0:T(4,128)}, f32[256]{0:T(256)}, /*index=5*/f32[16]{0:T(128)}, f32[16]{0:T(128)}, f32[16]{0:T(128)}, f32[1024]{0:T(1024)}) all-reduce(f32[512]{0:T(512)S(1)} %get-tuple-element.2138, ...), channel_id=1, replica_groups=mesh['batch'=4,'seq'=4,'head'=2] {'seq'}, use_global_device_ids=true, to_apply=%region_40.41 | all-reduce | flops 7984 | bytes 63872 | tf_op jit(solution)/shard_map/psum | solution.py:19
  785.2 419.3 %all-reduce.11.cloned.1.call-done = (f32[1024,1024]{1,0:T(8,128)}, f32[1024,1024]{1,0:T(8,128)}, f32[1024,16]{0,1:T(8,128)}, f32[1024,256]{1,0:T(8,128)}, f32[1024,1024]{1,0:T(8,128)}) async-done(((f32[1024,1024]{1,0:T(8,128)}, f32[1024,1024]{1,0:T(8,128)}, f32[1024,16]{0,1:T(8,128)}, f32[1024,256]{1,0:T(8,128)}, f32[1024,1024]{1,0:T(8,128)}), (f32[1024,1024]{1,0:T(8,128)}, f32[1024,1024]{1,0:T(8,128)}, ...) | async-done | bytes 13697040 | tf_op jit(solution)/shard_map/psum | solution.py:19
  1204.6 4.9 copy.562
  (605 shorter events, 211.5 us)
Async XLA Ops:
  7.2 173.2 %copy-start = (bf16[1024,1024]{1,0:T(8,128)(2,1)S(1)}, bf16[1024,1024]{1,0:T(8,128)(2,1)}, u32[]{:S(2)}) copy-start(bf16[1024,1024]{1,0:T(8,128)(2,1)} %param.28) | copy-start | bytes 6291460
  7.2 14.1 %all-gather.8.cloned.1.call-start = ((), (), s32[]{:S(2)}) async-start(), calls=%async_computation.2 | async-start | bytes 1572864 | tf_op jit(solution)/shard_map/all_gather | solution.py:139
  7.9 158.0 %all-gather.12.cloned.1.call-start = ((), (), s32[]{:S(2)}) async-start(), calls=%async_computation.6 | async-start | bytes 2621440 | tf_op jit(solution)/shard_map/all_gather | solution.py:31
  10.7 169.7 %copy-start.54 = (f32[2,1,512]{2,1,0:T(1,128)}, f32[2,1,512]{2,1,0:T(1,128)S(1)}, u32[]{:S(2)}) copy-start(f32[2,1,512]{2,1,0:T(1,128)S(1)} %convert_element_type.86) | copy-start | bytes 12292
  12.7 23.3 %copy-start.88 = (f32[1,256]{1,0:T(1,128)}, f32[1,256]{1,0:T(1,128)S(1)}, u32[]{:S(2)}) copy-start(f32[1,256]{1,0:T(1,128)S(1)} %get-tuple-element.2211) | copy-start | bytes 3076
  12.7 23.3 %copy-start.90 = (f32[1,256]{1,0:T(1,128)}, f32[1,256]{1,0:T(1,128)S(1)}, u32[]{:S(2)}) copy-start(f32[1,256]{1,0:T(1,128)S(1)} %get-tuple-element.2212) | copy-start | bytes 3076
  12.7 23.3 %copy-start.92 = (f32[1,256]{1,0:T(1,128)}, f32[1,256]{1,0:T(1,128)S(1)}, u32[]{:S(2)}) copy-start(f32[1,256]{1,0:T(1,128)S(1)} %get-tuple-element.2213) | copy-start | bytes 3076
  12.7 23.3 %copy-start.94 = (f32[1,256]{1,0:T(1,128)}, f32[1,256]{1,0:T(1,128)S(1)}, u32[]{:S(2)}) copy-start(f32[1,256]{1,0:T(1,128)S(1)} %get-tuple-element.2214) | copy-start | bytes 3076
  13.6 23.7 %copy-start.67 = (f32[1,1024]{1,0:T(1,128)}, f32[1,1024]{1,0:T(1,128)S(1)}, u32[]{:S(2)}) copy-start(f32[1,1024]{1,0:T(1,128)S(1)} %get-tuple-element.2207) | copy-start | bytes 12292
  13.6 23.7 %copy-start.69 = (f32[1,1024]{1,0:T(1,128)}, f32[1,1024]{1,0:T(1,128)S(1)}, u32[]{:S(2)}) copy-start(f32[1,1024]{1,0:T(1,128)S(1)} %get-tuple-element.2208) | copy-start | bytes 12292
  13.6 23.7 %copy-start.71 = (f32[1,1024]{1,0:T(1,128)}, f32[1,1024]{1,0:T(1,128)S(1)}, u32[]{:S(2)}) copy-start(f32[1,1024]{1,0:T(1,128)S(1)} %get-tuple-element.2209) | copy-start | bytes 12292
  13.6 23.7 %copy-start.73 = (f32[1,1024]{1,0:T(1,128)}, f32[1,1024]{1,0:T(1,128)S(1)}, u32[]{:S(2)}) copy-start(f32[1,1024]{1,0:T(1,128)S(1)} %get-tuple-element.2210) | copy-start | bytes 12292
  21.3 7.4 copy-start.24
  21.3 7.4 copy-start.41
  23.0 157.4 %copy-start.61 = (f32[512]{0:T(512)}, f32[512]{0:T(512)S(1)}, u32[]{:S(2)}) copy-start(f32[512]{0:T(512)S(1)} %add_rsqrt_fusion.1) | copy-start | bytes 6148
  24.9 11.2 copy-start.31
  24.9 9.9 copy-start.75
  24.9 9.9 copy-start.102
  24.9 11.1 collective-permute-start.1
  31.4 5.8 collective-permute-start
  50.0 72.3 %copy-start.99 = (f32[16]{0:T(128)S(1)}, f32[16]{0:T(128)}, u32[]{:S(2)}) copy-start(f32[16]{0:T(128)} %param.38) | copy-start | bytes 196
  120.8 67.6 %all-gather.10.cloned.1.call-start = ((), (), s32[]{:S(2)}) async-start(), calls=%async_computation.4 | async-start | bytes 1572864 | tf_op jit(solution)/shard_map/all_gather | solution.py:140
  121.5 162.5 %all-gather.14.cloned.1.call-start = ((), (), s32[]{:S(2)}) async-start(), calls=%async_computation.7 | async-start | bytes 2621440 | tf_op jit(solution)/shard_map/all_gather | solution.py:31
  180.4 8.0 copy-start.59
  188.3 8.4 copy-start.77
  196.7 7.9 copy-start.32
  213.4 227.6 %all-reduce.15.cloned.1.call-start = ((), (), s32[]{:S(2)}) async-start(), calls=%async_computation.10 | async-start | bytes 1048576 | tf_op jit(solution)/shard_map/psum | solution.py:220
  235.7 7.4 copy-start.49
  259.0 7.4 copy-start.49
  326.2 11.3 copy-start.85
  337.5 8.6 copy-start.86
  338.5 7.7 copy-start.5
  379.4 11.3 copy-start.85
  390.7 8.6 copy-start.86
  391.6 7.7 copy-start.5
  411.6 9.5 copy-start.58
  411.6 9.5 copy-start.57
  411.6 9.7 copy-start.25
  411.6 9.7 copy-start.63
  419.8 5.6 collective-permute-start.2
  421.3 289.5 %all-reduce.13.cloned.1.call-start = ((), (), s32[]{:S(2)}) async-start(), calls=%async_computation.9 | async-start | bytes 27394048 | tf_op jit(solution)/shard_map/psum | solution.py:19
  421.3 19.8 %copy-start.81 = (f32[1,3,256]{2,1,0:T(4,128)S(1)}, f32[1,3,256]{2,1,0:T(4,128)}, u32[]{:S(2)}) copy-start(f32[1,3,256]{2,1,0:T(4,128)} %copy-done.80) | copy-start | bytes 9220
  443.8 5.5 collective-permute-start.3
  451.1 272.1 %reduce-scatter.3.cloned.1.call-start = ((), (), s32[]{:S(2)}) async-start(), calls=%async_computation.3 | async-start | bytes 3145728 | tf_op jit(solution)/shard_map/reduce_scatter | solution.py:194
  456.7 279.8 %reduce-scatter.5.cloned.1.call-start = ((), (), s32[]{:S(2)}) async-start(), calls=%async_computation.5 | async-start | bytes 3145728 | tf_op jit(solution)/shard_map/reduce_scatter | solution.py:256
  463.4 741.2 %all-reduce.11.cloned.1.call-start = ((), (), s32[]{:S(2)}) async-start(), calls=%async_computation.8 | async-start | bytes 27394048 | tf_op jit(solution)/shard_map/psum | solution.py:19
  725.8 13.7 %copy-start.98 = (f32[1024]{0:T(1024)S(1)}, f32[1024]{0:T(1024)}, u32[]{:S(2)}) copy-start(f32[1024]{0:T(1024)} %get-tuple-element.1963) | copy-start | bytes 12292
  736.5 45.8 %copy-start.36 = (f32[512,512]{1,0:T(8,128)S(1)}, f32[512,512]{1,0:T(8,128)}, u32[]{:S(2)}) copy-start(f32[512,512]{1,0:T(8,128)} %reduce-scatter.5.cloned.1.call-done) | copy-start | bytes 3145732
  (112 other events, 430.0 us)
Sparse Core Ops, SparseCore 0:
  9.5 11.7 all-gather.7
  120.9 44.9 all-gather.11
  167.5 7.8 all-gather.9
  213.6 44.5 all-gather.13
  421.4 19.6 all-reduce.14
  451.3 259.4 all-reduce.12
  713.0 10.2 reduce-scatter.2
  725.5 10.8 reduce-scatter.4
  739.6 464.9 all-reduce.10
